TPU v7x, 128 devices: a whole 4x4x4 slice. The times are simulated.
128 devices in a mesh: ends: 2 (over z_hi), dp: 8 (over y, core), tp: 8 (over z_lo, x).
Axes of the slice: x: 4, y: 4, z: 4 (z_hi: 2, z_lo: 2; z = z_hi * 2 + z_lo), core: 2. Of those that a mesh axis runs over, the one named last changes fastest.
Arguments:
- grad: bfloat16 [2, 8, 16384, 3072], P('ends', 'dp', 'tp'), may hold values from -1800 to 1800
- master: float32 [8, 2048, 3072], P('tp', ('ends', 'dp')), may hold values from -3 to 3
- moment: float32 [8, 2048, 3072], P('tp', ('ends', 'dp')), may hold values from -3 to 3
- second: float32 [8, 2048, 3072], P('tp', ('ends', 'dp')), may hold values from 0.01 to 1
Outputs:
- weights: bfloat16 [16384, 3072], P('tp')
- master_out: float32 [8, 2048, 3072], P('tp', ('ends', 'dp'))
- moment_out: float32 [8, 2048, 3072], P('tp', ('ends', 'dp'))
- second_out: float32 [8, 2048, 3072], P('tp', ('ends', 'dp'))
All inputs are finite; a program needn't handle non-finite values.
Results may differ from a plain program's by a relative error of at most 0.0034.
Values may be sent and summed in bfloat16 or wider, within the bound.
No kernel may reach another device: no remote copies, remote signals or barrier semaphores. Data moves between devices by JAX's collectives and lax.ppermute only.
A program may use at most 128 MiB of HBM per device.

v0:
```python
import jax
import jax.numpy as jnp
from jax import lax
from jax.sharding import Mesh
from jax.sharding import PartitionSpec as P

STEP = 10
ENDS_DP = ("ends", "dp_0", "dp_1")
ENDS_DP_TP = ("ends", "dp_0", "dp_1", "tp_0", "tp_1")
TP = ("tp_0", "tp_1")
DP = ("dp_0", "dp_1")


def one_axis_at_a_time(x, axes):
    for axis in axes:
        x = lax.psum(x, axis)
    return x


def per_device(grad, master, moment, second):
    rows_tp = grad.shape[2]
    width = grad.shape[3]
    local = grad[0, 0].astype(jnp.float32)
    summed = lax.psum_scatter(
        local.astype(jnp.bfloat16), ENDS_DP, scatter_dimension=0, tiled=True
    ).astype(jnp.float32)
    squares = one_axis_at_a_time(jnp.sum(summed * summed), ENDS_DP_TP)
    vocab_total = rows_tp * lax.axis_size(TP)
    factor = jnp.minimum(
        jnp.float32(1.0), jnp.sqrt(jnp.float32(vocab_total * width)) / (jnp.sqrt(squares) + 1e-06)
    )
    clipped = factor * summed
    moment_out = 0.9 * moment[0] + 0.1 * clipped
    second_out = 0.999 * second[0] + 0.001 * clipped * clipped
    update = moment_out / (1.0 - 0.9**STEP) / (jnp.sqrt(second_out / (1.0 - 0.999**STEP)) + 1e-08)
    master_out = master[0] - 0.01 * (update + 0.1 * master[0])
    rounded = master_out.astype(jnp.bfloat16)
    weights = lax.all_gather(rounded, ENDS_DP, axis=0, tiled=True)
    return (weights, master_out[None], moment_out[None], second_out[None])


def solution(mesh):
    finer = Mesh(
        mesh.devices.reshape(mesh.shape["ends"], 4, 2, 2, 4),
        ("ends", "dp_0", "dp_1", "tp_0", "tp_1"),
    )
    return jax.shard_map(
        per_device,
        mesh=finer,
        in_specs=(
            P("ends", DP, TP, None),
            P(TP, ENDS_DP, None),
            P(TP, ENDS_DP, None),
            P(TP, ENDS_DP, None),
        ),
        out_specs=(P(TP, None), P(TP, ENDS_DP, None), P(TP, ENDS_DP, None), P(TP, ENDS_DP, None)),
        check_vma=False,
    )
```

profile of v0, /device:TPU:1, one launch (start us, length us, event | category | flops | bytes accessed | tf_op | source)
XLA Modules:
  0.0 287.3 jit_solution(16388377666645234331)
XLA Ops:
  7.2 0.0 reduce-scatter.2.cloned.1.call-start
  7.2 0.0 copy-start
  7.2 0.0 copy-start.1
  7.2 0.7 reduce-scatter.2.cloned.1.call-update
  7.9 0.0 all-gather.2.cloned.1.call-start
  7.9 129.3 %reduce-scatter.2.cloned.1.call-done = bf16[128,3072]{1,0:T(8,128)(2,1)} async-done(((bf16[2048,3072]{1,0:T(8,128)(2,1)}), bf16[128,3072]{1,0:T(8,128)(2,1)}) %reduce-scatter.2.cloned.1.call-update) | async-done | bytes 786448 | tf_op jit(solution)/shard_map/reduce_scatter | solution.py:24
  137.3 2.1 fusion.2
  139.4 5.9 %psum.35 = f32[]{:T(128)} all-reduce(f32[]{:T(128)} %fusion.2), channel_id=1, replica_groups=mesh['ends'=2,'dp_0'=4,'dp_1'=2,'tp_0'=2,'tp_1'=4] {'ends'}, use_global_device_ids=true, to_apply=%region_2.0 | all-reduce | flops 1 | bytes 8 | tf_op jit(solution)/shard_map/psum | solution.py:16
  145.3 7.5 %psum.36 = f32[]{:T(128)} all-reduce(f32[]{:T(128)} %psum.35), channel_id=1, replica_groups=mesh['ends'=2,'dp_0'=4,'dp_1'=2,'tp_0'=2,'tp_1'=4] {'dp_0'}, use_global_device_ids=true, to_apply=%region_3.0 | all-reduce | flops 1 | bytes 8 | tf_op jit(solution)/shard_map/psum | solution.py:16
  152.8 8.2 %psum.37 = f32[]{:T(128)} all-reduce(f32[]{:T(128)} %psum.36), channel_id=1, replica_groups=mesh['ends'=2,'dp_0'=4,'dp_1'=2,'tp_0'=2,'tp_1'=4] {'dp_1'}, use_global_device_ids=true, to_apply=%region_4.0 | all-reduce | flops 1 | bytes 8 | tf_op jit(solution)/shard_map/psum | solution.py:16
  161.0 4.4 %psum.38 = f32[]{:T(128)} all-reduce(f32[]{:T(128)} %psum.37), channel_id=1, replica_groups=mesh['ends'=2,'dp_0'=4,'dp_1'=2,'tp_0'=2,'tp_1'=4] {'tp_0'}, use_global_device_ids=true, to_apply=%region_5.0 | all-reduce | flops 1 | bytes 8 | tf_op jit(solution)/shard_map/psum | solution.py:16
  165.4 9.0 %psum.39 = f32[]{:T(128)} all-reduce(f32[]{:T(128)} %psum.38), channel_id=1, replica_groups=mesh['ends'=2,'dp_0'=4,'dp_1'=2,'tp_0'=2,'tp_1'=4] {'tp_1'}, use_global_device_ids=true, to_apply=%region_6.0 | all-reduce | flops 1 | bytes 8 | tf_op jit(solution)/shard_map/psum | solution.py:16
  175.1 0.0 copy-done
  175.2 0.0 copy-done.1
  175.2 5.4 %fusion.8 = (bf16[128,3072]{1,0:T(8,128)(2,1)}, f32[128,3072]{1,0:T(8,128)}, f32[1,128,3072]{2,1,0:T(8,128)}, f32[1,128,3072]{2,1,0:T(8,128)}) fusion(f32[1,128,3072]{2,1,0:T(8,128)S(1)} %copy-done, bf16[128,3072]{1,0:T(8,128)(2,1)} %reduce-scatter.2.cloned.1.call-done, f32[]{:T(128)S(6)} %min_shard_map.3, f32[1,128,3072]{2,1,0:T(8,128)S(1)} %copy-done.1, ...), kind=kLoop, calls=%fused_computation.13 | loop fusion | flops 7077888 | bytes 11010052 | tf_op jit(solution)/shard_map/convert_element_type | solution.py:37
  180.5 0.0 all-gather.2.cloned.1.call-update
  180.6 89.3 %all-gather.2.cloned.1.call-done = bf16[2048,3072]{1,0:T(8,128)(2,1)} async-done(((bf16[128,3072]{1,0:T(8,128)(2,1)}), bf16[2048,3072]{1,0:T(8,128)(2,1)}) %all-gather.2.cloned.1.call-update) | async-done | bytes 12582928 | tf_op jit(solution)/shard_map/all_gather | solution.py:38
  269.9 10.5 %copy.9 = bf16[2048,3072]{1,0:T(8,128)(2,1)} copy(bf16[2048,3072]{1,0:T(8,128)(2,1)} %all-gather.2.cloned.1.call-done) | data formatting | bytes 25165824
Async XLA Ops:
  7.2 130.1 %reduce-scatter.2.cloned.1.call-start = ((), (), s32[]{:S(2)}) async-start(), calls=%async_computation.1 | async-start | bytes 13369344 | tf_op jit(solution)/shard_map/reduce_scatter | solution.py:24
  7.2 167.9 %copy-start = (f32[1,128,3072]{2,1,0:T(8,128)S(1)}, f32[1,128,3072]{2,1,0:T(8,128)}, u32[]{:S(2)}) copy-start(f32[1,128,3072]{2,1,0:T(8,128)} %param.7) | copy-start | bytes 4718596
  7.2 167.9 %copy-start.1 = (f32[1,128,3072]{2,1,0:T(8,128)S(1)}, f32[1,128,3072]{2,1,0:T(8,128)}, u32[]{:S(2)}) copy-start(f32[1,128,3072]{2,1,0:T(8,128)} %param.6) | copy-start | bytes 4718596
  7.9 262.0 %all-gather.2.cloned.1.call-start = ((), (), s32[]{:S(2)}) async-start(), calls=%async_computation.2 | async-start | bytes 13369344 | tf_op jit(solution)/shard_map/all_gather | solution.py:38
Sparse Core Ops, SparseCore 0:
  12.4 124.8 reduce-scatter.1
  180.7 89.1 all-gather.1
where the time goes:
time: 288 us; the launch traced here: 287 us
  waiting for transfers between devices  219 us (76%)
  blocking collectives  35 us (12%)
  between operations  14.8 us (5%)
  local copies, waits for them, and re-layouts  10.5 us (4%)
  other arithmetic  7.52 us (3%)
    reduce_scatter x1, waiting for transfers between devices, per_device(): lax.psum_scatter(local.astype(jnp.bfloat16), ENDS_DP, scatter_dimension=0...  129 us
    all_gather x1, waiting for transfers between devices, per_device(): weights = lax.all_gather(rounded, ENDS_DP, axis=0, tiled=True)  89.3 us
    psum x5, blocking collectives, one_axis_at_a_time(): x = lax.psum(x, axis)  35 us
    unnamed x5, local copies, waits for them, and re-layouts  10.5 us
  transfers between devices with their start and end apart: 2, of which 2 were waited for; matrix products, arithmetic and copies ran while one was open for 0% of the time, Pallas kernels for 0%

commit v1 on v0

--- a/solution.py
+++ b/solution.py
@@ -35,7 +35,9 @@
     update = moment_out / (1.0 - 0.9**STEP) / (jnp.sqrt(second_out / (1.0 - 0.999**STEP)) + 1e-08)
     master_out = master[0] - 0.01 * (update + 0.1 * master[0])
     rounded = master_out.astype(jnp.bfloat16)
-    weights = lax.all_gather(rounded, ENDS_DP, axis=0, tiled=True)
+    weights = jnp.concatenate(
+        lax.all_to_all(jnp.stack([rounded] * lax.axis_size(ENDS_DP)), ENDS_DP, 0, 0), axis=0
+    )
     return (weights, master_out[None], moment_out[None], second_out[None])
 
 

time: 288 us -> 347 us (1.20)
  blocking collectives: 35 us -> 183 us
  waiting for transfers between devices: 219 us -> 130 us
    all_to_all x0 -> x1, blocking collectives: none -> 148 us  [per_device(): lax.all_to_all(jnp.stack([rounded] * lax.axis_size(ENDS_DP)), ENDS_DP, 0, 0)]
    all_gather x1 -> x0, waiting for transfers between devices: 89.3 us -> none  [per_device(): weights = lax.all_gather(rounded, ENDS_DP, axis=0, tiled=True)]
    another operation x0 -> x1, local copies, waits for them, and re-layouts: none -> 6.43 us  [per_device(): jnp.stack([rounded] * lax.axis_size(ENDS_DP))]
    unnamed x5 -> x3, local copies, waits for them, and re-layouts: 10.5 us -> 4.78 us
  transfers between devices with their start and end apart: 2 -> 1, of which waited for: 2 -> 1; matrix products, arithmetic and copies ran while one was open for 0% -> 0% of each run, Pallas kernels for 0% -> 0%
where the time goes in v1:
time: 347 us; the launch traced here: 346 us
  blocking collectives  183 us (53%)
  waiting for transfers between devices  130 us (37%)
  between operations  14.8 us (4%)
  local copies, waits for them, and re-layouts  11.2 us (3%)
  other arithmetic  7.29 us (2%)
    all_to_all x1, blocking collectives, per_device(): lax.all_to_all(jnp.stack([rounded] * lax.axis_size(ENDS_DP)), ENDS_DP, 0, 0)  148 us
    reduce_scatter x1, waiting for transfers between devices, per_device(): lax.psum_scatter(local.astype(jnp.bfloat16), ENDS_DP, scatter_dimension=0...  129 us
    psum x5, blocking collectives, one_axis_at_a_time(): x = lax.psum(x, axis)  35 us
  transfers between devices with their start and end apart: 1, of which 1 were waited for; matrix products, arithmetic and copies ran while one was open for 0% of the time, Pallas kernels for 0%

profile of v1, /device:TPU:1, one launch (start us, length us, event | category | flops | bytes accessed | tf_op | source)
XLA Modules:
  0.0 346.3 jit_solution(13866634823485664687)
XLA Ops:
  7.2 0.0 reduce-scatter.2.cloned.1.call-start
  7.2 0.0 copy-start
  7.2 0.7 reduce-scatter.2.cloned.1.call-update
  7.9 129.4 %reduce-scatter.2.cloned.1.call-done = bf16[128,3072]{1,0:T(8,128)(2,1)} async-done(((bf16[2048,3072]{1,0:T(8,128)(2,1)}), bf16[128,3072]{1,0:T(8,128)(2,1)}) %reduce-scatter.2.cloned.1.call-update) | async-done | bytes 786448 | tf_op jit(solution)/shard_map/reduce_scatter | solution.py:24
  137.3 2.1 fusion.2
  139.4 5.9 %psum.35 = f32[]{:T(128)} all-reduce(f32[]{:T(128)} %fusion.2), channel_id=1, replica_groups=mesh['ends'=2,'dp_0'=4,'dp_1'=2,'tp_0'=2,'tp_1'=4] {'ends'}, use_global_device_ids=true, to_apply=%region_2.0 | all-reduce | flops 1 | bytes 8 | tf_op jit(solution)/shard_map/psum | solution.py:16
  145.3 7.5 %psum.36 = f32[]{:T(128)} all-reduce(f32[]{:T(128)} %psum.35), channel_id=1, replica_groups=mesh['ends'=2,'dp_0'=4,'dp_1'=2,'tp_0'=2,'tp_1'=4] {'dp_0'}, use_global_device_ids=true, to_apply=%region_3.0 | all-reduce | flops 1 | bytes 8 | tf_op jit(solution)/shard_map/psum | solution.py:16
  152.8 8.2 %psum.37 = f32[]{:T(128)} all-reduce(f32[]{:T(128)} %psum.36), channel_id=1, replica_groups=mesh['ends'=2,'dp_0'=4,'dp_1'=2,'tp_0'=2,'tp_1'=4] {'dp_1'}, use_global_device_ids=true, to_apply=%region_4.0 | all-reduce | flops 1 | bytes 8 | tf_op jit(solution)/shard_map/psum | solution.py:16
  161.0 4.4 %psum.38 = f32[]{:T(128)} all-reduce(f32[]{:T(128)} %psum.37), channel_id=1, replica_groups=mesh['ends'=2,'dp_0'=4,'dp_1'=2,'tp_0'=2,'tp_1'=4] {'tp_0'}, use_global_device_ids=true, to_apply=%region_5.0 | all-reduce | flops 1 | bytes 8 | tf_op jit(solution)/shard_map/psum | solution.py:16
  165.4 9.0 %psum.39 = f32[]{:T(128)} all-reduce(f32[]{:T(128)} %psum.38), channel_id=1, replica_groups=mesh['ends'=2,'dp_0'=4,'dp_1'=2,'tp_0'=2,'tp_1'=4] {'tp_1'}, use_global_device_ids=true, to_apply=%region_6.0 | all-reduce | flops 1 | bytes 8 | tf_op jit(solution)/shard_map/psum | solution.py:16
  175.1 0.0 copy-done
  175.2 5.1 %fusion.8 = (bf16[128,3072]{1,0:T(8,128)(2,1)S(1)}, f32[128,3072]{1,0:T(8,128)}, f32[1,128,3072]{2,1,0:T(8,128)}, f32[1,128,3072]{2,1,0:T(8,128)}) fusion(f32[1,128,3072]{2,1,0:T(8,128)S(1)} %copy-done, bf16[128,3072]{1,0:T(8,128)(2,1)} %reduce-scatter.2.cloned.1.call-done, f32[]{:T(128)S(6)} %min_shard_map.3, f32[1,128,3072]{2,1,0:T(8,128)} %param.6, ...), kind=kLoop, calls=%fused_computation.13 | loop fusion | flops 7077888 | bytes 11010052 | tf_op jit(solution)/shard_map/convert_element_type | solution.py:37
  180.3 6.4 %stack.2 = bf16[16,128,3072]{2,1,0:T(8,128)(2,1)} broadcast(bf16[128,3072]{1,0:T(8,128)(2,1)S(1)} %get-tuple-element.4), dimensions={1,2} | broadcast | bytes 13369344 | tf_op jit(solution)/shard_map/stack | solution.py:39
  186.7 147.9 %all_to_all.5 = bf16[16,128,3072]{2,1,0:T(8,128)(2,1)S(1)} all-to-all(bf16[16,128,3072]{2,1,0:T(8,128)(2,1)} %stack.2), channel_id=1, replica_groups=mesh['ends'=2,'dp_0'=4,'dp_1'=2,'tp_0'=2,'tp_1'=4] {'ends','dp_0','dp_1'}, dimensions={0} | all-to-all | bytes 25165824 | tf_op jit(solution)/shard_map/all_to_all | solution.py:39
  334.7 4.8 %copy.9 = bf16[2048,3072]{1,0:T(8,128)(2,1)} copy(bf16[2048,3072]{1,0:T(8,128)(2,1)S(1)} %bitcast.31) | data formatting | bytes 25165824
Async XLA Ops:
  7.2 130.1 %reduce-scatter.2.cloned.1.call-start = ((), (), s32[]{:S(2)}) async-start(), calls=%async_computation.2 | async-start | bytes 13369344 | tf_op jit(solution)/shard_map/reduce_scatter | solution.py:24
  7.2 167.9 %copy-start = (f32[1,128,3072]{2,1,0:T(8,128)S(1)}, f32[1,128,3072]{2,1,0:T(8,128)}, u32[]{:S(2)}) copy-start(f32[1,128,3072]{2,1,0:T(8,128)} %param.7) | copy-start | bytes 4718596
Sparse Core Ops, SparseCore 0:
  12.4 124.8 reduce-scatter.1

commit v2 on v0

--- a/solution.py
+++ b/solution.py
@@ -13,7 +13,7 @@
 
 def one_axis_at_a_time(x, axes):
     for axis in axes:
-        x = lax.psum(x, axis)
+        x = jnp.sum(lax.all_gather(x, axis), axis=0)
     return x
 
 

time: 288 us -> 297 us (1.031)
  local copies, waits for them, and re-layouts: 10.5 us -> 20.5 us
  blocking collectives: 35 us -> 31.8 us
  other arithmetic: 7.52 us -> 10.5 us
    psum x5 -> x0, blocking collectives: 35 us -> none  [one_axis_at_a_time(): x = lax.psum(x, axis)]
    unnamed x0 -> x5, blocking collectives: none -> 31.8 us
    unnamed x5 -> x30, local copies, waits for them, and re-layouts: 10.5 us -> 20.5 us
    reduce_sum x0 -> x5, other arithmetic: none -> 3.02 us  [one_axis_at_a_time(): x = jnp.sum(lax.all_gather(x, axis), axis=0)]
where the time goes in v2:
time: 297 us
  waiting for transfers between devices  219 us (74%)
  blocking collectives  31.8 us (11%)
  local copies, waits for them, and re-layouts  20.5 us (7%)
  between operations  14.9 us (5%)
  other arithmetic  10.5 us (4%)
    reduce_scatter x1, waiting for transfers between devices, per_device(): lax.psum_scatter(local.astype(jnp.bfloat16), ENDS_DP, scatter_dimension=0...  129 us
    all_gather x1, waiting for transfers between devices, per_device(): weights = lax.all_gather(rounded, ENDS_DP, axis=0, tiled=True)  89.3 us
    unnamed x5, blocking collectives  31.8 us
    unnamed x30, local copies, waits for them, and re-layouts  20.5 us
  transfers between devices with their start and end apart: 2, of which 2 were waited for; matrix products, arithmetic and copies ran while one was open for 0% of the time, Pallas kernels for 0%

profile of v2, /device:TPU:1, one launch (start us, length us, event | category | flops | bytes accessed | tf_op | source)
XLA Modules:
  0.0 296.5 jit_solution(14974217170417070856)
XLA Ops:
  7.2 0.0 reduce-scatter.2.cloned.1.call-start
  7.2 0.0 copy-start.6
  7.2 0.0 copy-start.5
  7.2 0.0 copy-start.4
  7.2 0.0 copy-start.3
  7.3 0.0 copy-start.2
  7.3 0.0 copy-start
  7.3 0.0 copy-start.1
  7.3 0.6 reduce-scatter.2.cloned.1.call-update
  7.9 0.0 all-gather.2.cloned.1.call-start
  8.0 0.0 copy-done.6
  8.0 0.6 dynamic-slice
  8.5 128.7 %reduce-scatter.2.cloned.1.call-done = bf16[128,3072]{1,0:T(8,128)(2,1)} async-done(((bf16[2048,3072]{1,0:T(8,128)(2,1)}), bf16[128,3072]{1,0:T(8,128)(2,1)}) %reduce-scatter.2.cloned.1.call-update) | async-done | bytes 786448 | tf_op jit(solution)/shard_map/reduce_scatter | solution.py:24
  137.3 2.1 fusion.2
  139.4 1.4 dynamic-update-slice
  140.8 0.0 copy-done.5
  140.8 0.6 dynamic-slice.1
  141.4 5.3 %all-reduce = f32[2]{0:T(128)S(1)} all-reduce(f32[2]{0:T(128)S(1)} %dynamic-update-slice), channel_id=1, replica_groups=mesh['ends'=2,'dp_0'=4,'dp_1'=2,'tp_0'=2,'tp_1'=4] {'ends'}, use_global_device_ids=true, to_apply=%add | all-reduce | flops 2 | bytes 16
  146.7 0.6 reduce_sum.55
  147.3 1.4 dynamic-update-slice.1
  148.7 0.0 copy-done.4
  148.7 0.6 dynamic-slice.2
  149.3 6.9 %all-reduce.1 = f32[4]{0:T(128)S(1)} all-reduce(f32[4]{0:T(128)S(1)} %dynamic-update-slice.1), channel_id=1, replica_groups=mesh['ends'=2,'dp_0'=4,'dp_1'=2,'tp_0'=2,'tp_1'=4] {'dp_0'}, use_global_device_ids=true, to_apply=%add.1 | all-reduce | flops 4 | bytes 32
  156.1 0.6 reduce_sum.56
  156.7 1.4 dynamic-update-slice.2
  158.1 0.0 copy-done.3
  158.1 0.6 dynamic-slice.3
  158.7 7.5 %all-reduce.2 = f32[2]{0:T(128)S(1)} all-reduce(f32[2]{0:T(128)S(1)} %dynamic-update-slice.2), channel_id=1, replica_groups=mesh['ends'=2,'dp_0'=4,'dp_1'=2,'tp_0'=2,'tp_1'=4] {'dp_1'}, use_global_device_ids=true, to_apply=%add.2 | all-reduce | flops 2 | bytes 16
  166.3 0.6 reduce_sum.57
  166.9 1.4 dynamic-update-slice.3
  168.3 0.0 copy-done.2
  168.3 0.6 dynamic-slice.4
  168.9 3.8 %all-reduce.3 = f32[2]{0:T(128)S(1)} all-reduce(f32[2]{0:T(128)S(1)} %dynamic-update-slice.3), channel_id=1, replica_groups=mesh['ends'=2,'dp_0'=4,'dp_1'=2,'tp_0'=2,'tp_1'=4] {'tp_0'}, use_global_device_ids=true, to_apply=%add.3 | all-reduce | flops 2 | bytes 16
  172.6 0.6 reduce_sum.58
  173.2 1.4 dynamic-update-slice.4
  174.6 8.4 %all-reduce.4 = f32[4]{0:T(128)S(1)} all-reduce(f32[4]{0:T(128)S(1)} %dynamic-update-slice.4), channel_id=1, replica_groups=mesh['ends'=2,'dp_0'=4,'dp_1'=2,'tp_0'=2,'tp_1'=4] {'tp_1'}, use_global_device_ids=true, to_apply=%add.4 | all-reduce | flops 4 | bytes 32
  183.0 0.6 reduce_sum.59
  184.4 0.0 copy-done
  184.4 0.0 copy-done.1
  184.4 5.4 %fusion.8 = (bf16[128,3072]{1,0:T(8,128)(2,1)}, f32[128,3072]{1,0:T(8,128)}, f32[1,128,3072]{2,1,0:T(8,128)}, f32[1,128,3072]{2,1,0:T(8,128)}) fusion(f32[1,128,3072]{2,1,0:T(8,128)S(1)} %copy-done, bf16[128,3072]{1,0:T(8,128)(2,1)} %reduce-scatter.2.cloned.1.call-done, f32[]{:T(128)S(6)} %min_shard_map.3, f32[1,128,3072]{2,1,0:T(8,128)S(1)} %copy-done.1, ...), kind=kLoop, calls=%fused_computation.13 | loop fusion | flops 7077888 | bytes 11010052 | tf_op jit(solution)/shard_map/convert_element_type | solution.py:37
  189.8 0.0 all-gather.2.cloned.1.call-update
  189.8 89.3 %all-gather.2.cloned.1.call-done = bf16[2048,3072]{1,0:T(8,128)(2,1)} async-done(((bf16[128,3072]{1,0:T(8,128)(2,1)}), bf16[2048,3072]{1,0:T(8,128)(2,1)}) %all-gather.2.cloned.1.call-update) | async-done | bytes 12582928 | tf_op jit(solution)/shard_map/all_gather | solution.py:38
  279.1 10.5 %copy.19 = bf16[2048,3072]{1,0:T(8,128)(2,1)} copy(bf16[2048,3072]{1,0:T(8,128)(2,1)} %all-gather.2.cloned.1.call-done) | data formatting | bytes 25165824
  (5 shorter events, 0.0 us)
Async XLA Ops:
  7.2 130.1 %reduce-scatter.2.cloned.1.call-start = ((), (), s32[]{:S(2)}) async-start(), calls=%async_computation.1 | async-start | bytes 13369344 | tf_op jit(solution)/shard_map/reduce_scatter | solution.py:24
  7.2 0.7 copy-start.6
  7.2 133.6 %copy-start.5 = (u32[128]{0:T(128)S(1)}, u32[128]{0:T(128)}, u32[]{:S(2)}) copy-start(u32[128]{0:T(128)} %constant.37) | copy-start | bytes 1540
  7.2 141.4 %copy-start.4 = (u32[128]{0:T(128)S(1)}, u32[128]{0:T(128)}, u32[]{:S(2)}) copy-start(u32[128]{0:T(128)} %constant.42) | copy-start | bytes 1540
  7.2 150.9 %copy-start.3 = (u32[128]{0:T(128)S(1)}, u32[128]{0:T(128)}, u32[]{:S(2)}) copy-start(u32[128]{0:T(128)} %constant.47) | copy-start | bytes 1540
  7.3 161.0 %copy-start.2 = (u32[128]{0:T(128)S(1)}, u32[128]{0:T(128)}, u32[]{:S(2)}) copy-start(u32[128]{0:T(128)} %constant.52) | copy-start | bytes 1540
  7.3 177.1 %copy-start = (f32[1,128,3072]{2,1,0:T(8,128)S(1)}, f32[1,128,3072]{2,1,0:T(8,128)}, u32[]{:S(2)}) copy-start(f32[1,128,3072]{2,1,0:T(8,128)} %param.7) | copy-start | bytes 4718596
  7.3 177.1 %copy-start.1 = (f32[1,128,3072]{2,1,0:T(8,128)S(1)}, f32[1,128,3072]{2,1,0:T(8,128)}, u32[]{:S(2)}) copy-start(f32[1,128,3072]{2,1,0:T(8,128)} %param.6) | copy-start | bytes 4718596
  7.9 271.2 %all-gather.2.cloned.1.call-start = ((), (), s32[]{:S(2)}) async-start(), calls=%async_computation.2 | async-start | bytes 13369344 | tf_op jit(solution)/shard_map/all_gather | solution.py:38
Sparse Core Ops, SparseCore 0:
  12.4 124.8 reduce-scatter.1
  189.9 89.1 all-gather.1
